TPU v7x, 32 devices: a whole 2x2x4 slice. The times are simulated.
32 devices in a mesh: seq: 8 (over z, y), ch: 4 (over x, core).
Axes of the slice: x: 2, y: 2, z: 4, core: 2. Of those that a mesh axis runs over, the one named last changes fastest.
Arguments:
- queries: float32 [1024, 1024], P('seq', 'ch'), may hold values from -6 to 6
- keys: float32 [1024, 1024], P('seq', 'ch'), may hold values from -6 to 6
- values: float32 [1024, 1024], P('seq', 'ch'), may hold values from -6 to 6
- filters: float32 [1024, 1024], P('seq', 'ch'), may hold values from -0.375 to 0.375
- short_w: float32 [3, 1024], P(None, 'ch'), may hold values from -3.5 to 3.5
- bias: float32 [1024], P('ch'), may hold values from -4 to 4
Outputs:
- mixed: float32 [1024, 1024], P('seq', 'ch')
All inputs are finite; a program needn't handle non-finite values.
Results may differ from a plain program's by a relative error of at most 0.00011.
Values sent between devices are 32-bit elements; how exact they have to be, the bound alone decides.
A program may use at most 64 MiB of HBM per device.

v0:
```python
import math
import jax
import jax.numpy as jnp
from jax import lax
from jax.sharding import PartitionSpec as P


def passed_along(block, axis, distance):
    devices = range(lax.axis_size(axis))
    route = [(i - distance, i) for i in devices if i - distance in devices]
    return lax.ppermute(block, axis, route)


def angles(index, modulus, sign):
    turned = (index % modulus).astype(jnp.float32) * (2.0 * math.pi / modulus)
    return (jnp.cos(turned), sign * jnp.sin(turned))


def complex_mix(form, mat_real, mat_imag, data_real, data_imag):
    first = jnp.einsum(form, mat_real, data_real, precision=lax.Precision.HIGHEST)
    second = jnp.einsum(form, mat_imag, data_imag, precision=lax.Precision.HIGHEST)
    third = jnp.einsum(form, mat_real, data_imag, precision=lax.Precision.HIGHEST)
    fourth = jnp.einsum(form, mat_imag, data_real, precision=lax.Precision.HIGHEST)
    return (first - second, third + fourth)


def body(queries, keys, values, filters, short_w, bias):
    row_count, channels = queries.shape
    shards = lax.axis_size("seq")
    device = lax.axis_index("seq")
    slab = row_count // shards
    total = row_count * shards
    stacked = jnp.stack((queries, keys, values))
    earlier = passed_along(stacked[:, row_count - 2 :, :], "seq", 1)
    extended = jnp.concatenate((earlier, stacked), axis=1)
    shorted = (
        short_w[0] * extended[:, 2:]
        + short_w[1] * extended[:, 1:-1]
        + short_w[2] * extended[:, :-2]
    )
    gated = shorted[1] * shorted[2]
    signal = jnp.stack((gated, filters))
    within = device * slab + jnp.arange(slab, dtype=jnp.int32)
    column_index = jnp.arange(shards, dtype=jnp.int32)
    row_index = jnp.arange(row_count, dtype=jnp.int32)
    own_pos = row_count * device + row_index
    cosine, sine = angles(own_pos, 2 * total, -1.0)
    lifted = jnp.stack((signal, signal * cosine[:, None], signal * sine[:, None]), axis=1)[
        :, :, None
    ]
    received = lax.all_to_all(lifted, "seq", split_axis=3, concat_axis=2, tiled=True)
    real_part = jnp.stack((received[:, 0], received[:, 1]), axis=1)
    imag_part = jnp.stack((jnp.zeros_like(received[:, 0]), received[:, 2]), axis=1)
    freq_cos, freq_sin = angles(column_index[:, None] * column_index[None, :], shards, -1.0)
    real_part, imag_part = complex_mix("kd,srdmc->srkmc", freq_cos, freq_sin, real_part, imag_part)
    twist_cos, twist_sin = angles(column_index[:, None] * within[None, :], total, -1.0)
    twist_cos = twist_cos[:, :, None]
    twist_sin = twist_sin[:, :, None]
    real_part, imag_part = (
        real_part * twist_cos - imag_part * twist_sin,
        real_part * twist_sin + imag_part * twist_cos,
    )
    square_index = row_index[:, None] * row_index[None, :]
    long_cos, long_sin = angles(square_index, row_count, -1.0)
    pair = (
        lax.all_to_all(real_part, "seq", split_axis=2, concat_axis=3, tiled=True),
        lax.all_to_all(imag_part, "seq", split_axis=2, concat_axis=3, tiled=True),
    )
    spec_real, spec_imag = complex_mix("km,srjmc->srjkc", long_cos, long_sin, pair[0], pair[1])
    prod_real = spec_real[0] * spec_real[1] - spec_imag[0] * spec_imag[1]
    prod_imag = spec_real[0] * spec_imag[1] + spec_imag[0] * spec_real[1]
    inverse_cos, inverse_sin = angles(square_index, row_count, 1.0)
    back_real, back_imag = complex_mix(
        "mk,rjkc->rjmc", inverse_cos, inverse_sin, prod_real, prod_imag
    )
    undo_cos, undo_sin = angles(device * row_index, total, 1.0)
    undo_cos = undo_cos[:, None]
    undo_sin = undo_sin[:, None]
    back_real, back_imag = (
        back_real * undo_cos - back_imag * undo_sin,
        back_real * undo_sin + back_imag * undo_cos,
    )
    column_cos, column_sin = angles(column_index[:, None] * column_index[None, :], shards, 1.0)
    pair = (
        lax.all_to_all(back_real, "seq", split_axis=2, concat_axis=1, tiled=True),
        lax.all_to_all(back_imag, "seq", split_axis=2, concat_axis=1, tiled=True),
    )
    inv_real, inv_imag = complex_mix("dk,rkmc->rdmc", column_cos, column_sin, pair[0], pair[1])
    factor = 0.5 / total
    packed = jnp.stack((inv_real[0], inv_imag[0], inv_real[1], inv_imag[1]))
    landed = lax.all_to_all(packed, "seq", split_axis=1, concat_axis=2, tiled=True)
    cosine, sine = angles(own_pos, 2 * total, 1.0)
    long_part = factor * (
        landed[0, 0] + cosine[:, None] * landed[2, 0] - sine[:, None] * landed[3, 0]
    )
    return shorted[0] * (long_part + bias * gated)


def solution(mesh):
    placed = (
        P("seq", "ch"),
        P("seq", "ch"),
        P("seq", "ch"),
        P("seq", "ch"),
        P(None, "ch"),
        P("ch"),
    )
    return jax.shard_map(
        body, mesh=mesh, in_specs=placed, out_specs=P("seq", "ch"), check_vma=False
    )
```

profile of v0, /device:TPU:0, one launch (start us, length us, event | category | flops | bytes accessed | tf_op | source)
XLA Modules:
  0.0 130.0 jit_solution(9830155882568192317)
XLA Ops:
  0.0 1.1 pad_maximum_fusion.1
  1.1 4.9 %collective-permute-start = (f32[3,2,256]{2,1,0:T(2,128)S(1)}, f32[3,2,256]{2,1,0:T(2,128)S(1)}, u32[]{:S(2)}, u32[]{:S(2)}) collective-permute-start(f32[3,2,256]{2,1,0:T(2,128)S(1)} %slice.95), channel_id=1, source_target_pairs={{0,4},{4,8},{8,12},{12,16},{16,20},{20,24},{24,28},{1,5},{5,9},{9,... | collective-permute-start | bytes 18440 | tf_op jit(solution)/shard_map/ppermute | solution.py:11
  6.2 1.2 collective-permute-done
  8.7 1.5 %copy.53 = f32[2,3,1,128,256]{4,0,2,1,3:T(2,128)} copy(f32[2,3,1,128,256]{4,3,1,0,2:T(8,128)S(1)} %maximum_bitcast_fusion) | data formatting | bytes 1572864 | tf_op jit(solution)/shard_map/broadcast_in_dim | solution.py:48
  10.2 6.6 %all-to-all-start = ((f32[2,3,1,128,256]{4,0,2,1,3:T(2,128)}), f32[2,3,1,128,256]{4,0,2,1,3:T(2,128)S(1)}, u32[]{:S(2)}, u32[]{:S(2)}) async-start(f32[2,3,1,128,256]{4,0,2,1,3:T(2,128)} %copy.53), calls=%async_computation | async-start | bytes 1572864 | tf_op jit(solution)/shard_map/all_to_all | solution.py:51
  16.9 19.0 %all-to-all-done = f32[2,3,1,128,256]{4,0,2,1,3:T(2,128)S(1)} async-done(((f32[2,3,1,128,256]{4,0,2,1,3:T(2,128)}), f32[2,3,1,128,256]{4,0,2,1,3:T(2,128)S(1)}, u32[]{:S(2)}, u32[]{:S(2)}) %all-to-all-start) | async-done | bytes 786464 | tf_op jit(solution)/shard_map/all_to_all | solution.py:51
  36.9 0.9 fusion.8
  39.3 1.0 copy.57
  40.3 3.5 %all-to-all-start.1 = ((f32[2,2,8,16,256]{4,3,1,0,2:T(8,128)}), f32[2,2,8,16,256]{4,3,1,0,2:T(8,128)S(1)}, u32[]{:S(2)}, u32[]{:S(2)}) async-start(f32[2,2,8,16,256]{4,3,1,0,2:T(8,128)} %copy.57), calls=%async_computation.1 | async-start | bytes 1048576 | tf_op jit(solution)/shard_map/all_to_all | solution.py:66
  43.8 1.0 copy.60
  44.8 13.4 %all-to-all-done.1 = f32[2,2,8,16,256]{4,3,1,0,2:T(8,128)S(1)} async-done(((f32[2,2,8,16,256]{4,3,1,0,2:T(8,128)}), f32[2,2,8,16,256]{4,3,1,0,2:T(8,128)S(1)}, u32[]{:S(2)}, u32[]{:S(2)}) %all-to-all-start.1) | async-done | bytes 524320 | tf_op jit(solution)/shard_map/all_to_all | solution.py:66
  58.2 3.7 %all-to-all-start.2 = ((f32[2,2,8,16,256]{4,3,1,0,2:T(8,128)}), f32[2,2,8,16,256]{4,3,1,0,2:T(8,128)S(1)}, u32[]{:S(2)}, u32[]{:S(2)}) async-start(f32[2,2,8,16,256]{4,3,1,0,2:T(8,128)} %copy.60), calls=%async_computation.2 | async-start | bytes 1048576 | tf_op jit(solution)/shard_map/all_to_all | solution.py:67
  62.0 1.1 fusion.46
  63.1 13.4 %all-to-all-done.2 = f32[2,2,8,16,256]{4,3,1,0,2:T(8,128)S(1)} async-done(((f32[2,2,8,16,256]{4,3,1,0,2:T(8,128)}), f32[2,2,8,16,256]{4,3,1,0,2:T(8,128)S(1)}, u32[]{:S(2)}, u32[]{:S(2)}) %all-to-all-start.2) | async-done | bytes 524320 | tf_op jit(solution)/shard_map/all_to_all | solution.py:67
  76.5 1.1 fusion.44
  77.6 1.1 fusion.3
  78.8 1.1 fusion.2
  83.3 3.6 %all-to-all-start.3 = ((f32[2,1,128,256]{3,0,1,2:T(2,128)}), f32[2,1,128,256]{3,0,1,2:T(2,128)S(1)}, u32[]{:S(2)}, u32[]{:S(2)}) async-start(f32[2,1,128,256]{3,0,1,2:T(2,128)} %copy.65), calls=%async_computation.3 | async-start | bytes 524288 | tf_op jit(solution)/shard_map/all_to_all | solution.py:85
  87.8 8.2 %all-to-all-done.3 = f32[2,1,128,256]{3,0,1,2:T(2,128)S(1)} async-done(((f32[2,1,128,256]{3,0,1,2:T(2,128)}), f32[2,1,128,256]{3,0,1,2:T(2,128)S(1)}, u32[]{:S(2)}, u32[]{:S(2)}) %all-to-all-start.3) | async-done | bytes 262176 | tf_op jit(solution)/shard_map/all_to_all | solution.py:85
  96.0 3.6 %all-to-all-start.4 = ((f32[2,1,128,256]{3,0,1,2:T(2,128)}), f32[2,1,128,256]{3,0,1,2:T(2,128)S(1)}, u32[]{:S(2)}, u32[]{:S(2)}) async-start(f32[2,1,128,256]{3,0,1,2:T(2,128)} %copy.68), calls=%async_computation.4 | async-start | bytes 524288 | tf_op jit(solution)/shard_map/all_to_all | solution.py:86
  100.2 8.0 %all-to-all-done.4 = f32[2,1,128,256]{3,0,1,2:T(2,128)S(1)} async-done(((f32[2,1,128,256]{3,0,1,2:T(2,128)}), f32[2,1,128,256]{3,0,1,2:T(2,128)S(1)}, u32[]{:S(2)}, u32[]{:S(2)}) %all-to-all-start.4) | async-done | bytes 262176 | tf_op jit(solution)/shard_map/all_to_all | solution.py:86
  109.9 1.0 copy.73
  110.8 3.6 %all-to-all-start.5 = ((f32[4,8,16,256]{3,2,0,1:T(8,128)}), f32[4,8,16,256]{3,2,0,1:T(8,128)S(1)}, u32[]{:S(2)}, u32[]{:S(2)}) async-start(f32[4,8,16,256]{3,2,0,1:T(8,128)} %copy.73), calls=%async_computation.5 | async-start | bytes 1048576 | tf_op jit(solution)/shard_map/all_to_all | solution.py:91
  114.5 14.1 %all-to-all-done.5 = f32[4,8,16,256]{3,2,0,1:T(8,128)S(1)} async-done(((f32[4,8,16,256]{3,2,0,1:T(8,128)}), f32[4,8,16,256]{3,2,0,1:T(8,128)S(1)}, u32[]{:S(2)}, u32[]{:S(2)}) %all-to-all-start.5) | async-done | bytes 524320 | tf_op jit(solution)/shard_map/all_to_all | solution.py:91
  (53 shorter events, 12.0 us)
Async XLA Ops:
  0.0 7.4 %copy-start = (f32[128,256]{1,0:T(8,128)S(1)}, f32[128,256]{1,0:T(8,128)}, u32[]{:S(2)}) copy-start(f32[128,256]{1,0:T(8,128)} %param.8) | copy-start | bytes 393220
  0.0 7.4 %copy-start.1 = (f32[128,256]{1,0:T(8,128)S(1)}, f32[128,256]{1,0:T(8,128)}, u32[]{:S(2)}) copy-start(f32[128,256]{1,0:T(8,128)} %param.7) | copy-start | bytes 393220
  0.0 7.4 %copy-start.2 = (f32[128,256]{1,0:T(8,128)S(1)}, f32[128,256]{1,0:T(8,128)}, u32[]{:S(2)}) copy-start(f32[128,256]{1,0:T(8,128)} %param.6) | copy-start | bytes 393220
  1.1 4.9 %copy-start.4 = (f32[3,256]{1,0:T(4,128)S(1)}, f32[3,256]{1,0:T(4,128)}, u32[]{:S(2)}) copy-start(f32[3,256]{1,0:T(4,128)} %param.10) | copy-start | bytes 9220
  1.1 6.2 %collective-permute-start = (f32[3,2,256]{2,1,0:T(2,128)S(1)}, f32[3,2,256]{2,1,0:T(2,128)S(1)}, u32[]{:S(2)}, u32[]{:S(2)}) collective-permute-start(f32[3,2,256]{2,1,0:T(2,128)S(1)} %slice.95), channel_id=1, source_target_pairs={{0,4},{4,8},{8,12},{12,16},{16,20},{20,24},{24,28},{1,5},{5,9},{9,... | collective-permute-start | bytes 18440 | tf_op jit(solution)/shard_map/ppermute | solution.py:11
  7.6 0.9 copy-start.3
  10.2 25.7 %all-to-all-start = ((f32[2,3,1,128,256]{4,0,2,1,3:T(2,128)}), f32[2,3,1,128,256]{4,0,2,1,3:T(2,128)S(1)}, u32[]{:S(2)}, u32[]{:S(2)}) async-start(f32[2,3,1,128,256]{4,0,2,1,3:T(2,128)} %copy.53), calls=%async_computation | async-start | bytes 1572864 | tf_op jit(solution)/shard_map/all_to_all | solution.py:51
  40.3 17.9 %all-to-all-start.1 = ((f32[2,2,8,16,256]{4,3,1,0,2:T(8,128)}), f32[2,2,8,16,256]{4,3,1,0,2:T(8,128)S(1)}, u32[]{:S(2)}, u32[]{:S(2)}) async-start(f32[2,2,8,16,256]{4,3,1,0,2:T(8,128)} %copy.57), calls=%async_computation.1 | async-start | bytes 1048576 | tf_op jit(solution)/shard_map/all_to_all | solution.py:66
  58.2 18.3 %all-to-all-start.2 = ((f32[2,2,8,16,256]{4,3,1,0,2:T(8,128)}), f32[2,2,8,16,256]{4,3,1,0,2:T(8,128)S(1)}, u32[]{:S(2)}, u32[]{:S(2)}) async-start(f32[2,2,8,16,256]{4,3,1,0,2:T(8,128)} %copy.60), calls=%async_computation.2 | async-start | bytes 1048576 | tf_op jit(solution)/shard_map/all_to_all | solution.py:67
  83.3 12.7 %all-to-all-start.3 = ((f32[2,1,128,256]{3,0,1,2:T(2,128)}), f32[2,1,128,256]{3,0,1,2:T(2,128)S(1)}, u32[]{:S(2)}, u32[]{:S(2)}) async-start(f32[2,1,128,256]{3,0,1,2:T(2,128)} %copy.65), calls=%async_computation.3 | async-start | bytes 524288 | tf_op jit(solution)/shard_map/all_to_all | solution.py:85
  96.0 12.2 %all-to-all-start.4 = ((f32[2,1,128,256]{3,0,1,2:T(2,128)}), f32[2,1,128,256]{3,0,1,2:T(2,128)S(1)}, u32[]{:S(2)}, u32[]{:S(2)}) async-start(f32[2,1,128,256]{3,0,1,2:T(2,128)} %copy.68), calls=%async_computation.4 | async-start | bytes 524288 | tf_op jit(solution)/shard_map/all_to_all | solution.py:86
  110.8 17.7 %all-to-all-start.5 = ((f32[4,8,16,256]{3,2,0,1:T(8,128)}), f32[4,8,16,256]{3,2,0,1:T(8,128)S(1)}, u32[]{:S(2)}, u32[]{:S(2)}) async-start(f32[4,8,16,256]{3,2,0,1:T(8,128)} %copy.73), calls=%async_computation.5 | async-start | bytes 1048576 | tf_op jit(solution)/shard_map/all_to_all | solution.py:91
  128.6 0.7 copy-start.5
where the time goes:
time: 131 us; the launch traced here: 130 us
  waiting for transfers between devices  77.2 us (59%)
  starting transfers between devices  29.5 us (23%)
  matrix products  12.3 us (9%)
  local copies, waits for them, and re-layouts  7.97 us (6%)
  other arithmetic  2.65 us (2%)
    all_to_all x1, waiting for transfers between devices, body(): lax.all_to_all(lifted, 'seq', split_axis=3, concat_axis=2, tiled=True)  19 us
    all_to_all x1, waiting for transfers between devices, body(): lax.all_to_all(packed, 'seq', split_axis=1, concat_axis=2, tiled=True)  14.1 us
    all_to_all x1, waiting for transfers between devices, body(): lax.all_to_all(real_part, 'seq', split_axis=2, concat_axis=3, tiled=True)  13.4 us
    all_to_all x1, waiting for transfers between devices, body(): lax.all_to_all(imag_part, 'seq', split_axis=2, concat_axis=3, tiled=True)  13.4 us
    all_to_all x1, waiting for transfers between devices, body(): lax.all_to_all(back_real, 'seq', split_axis=2, concat_axis=1, tiled=True)  8.24 us
    all_to_all x1, waiting for transfers between devices, body(): lax.all_to_all(back_imag, 'seq', split_axis=2, concat_axis=1, tiled=True)  8.02 us
    all_to_all x1, starting transfers between devices, body(): lax.all_to_all(lifted, 'seq', split_axis=3, concat_axis=2, tiled=True)  6.6 us
    ppermute x1, starting transfers between devices, passed_along(): return lax.ppermute(block, axis, route)  4.9 us
  transfers between devices with their start and end apart: 7, of which 7 were waited for; matrix products, arithmetic and copies ran while one was open for 3% of the time, Pallas kernels for 0%

commit v1 on v0

--- a/solution.py
+++ b/solution.py
@@ -3,6 +3,28 @@
 import jax.numpy as jnp
 from jax import lax
 from jax.sharding import PartitionSpec as P
+
+
+def cut_along(x, dim, count):
+    before, after = (x.shape[:dim], x.shape[dim + 1 :])
+    return jnp.moveaxis(x.reshape(*before, count, -1, *after), dim, 0)
+
+
+def joined_along(pieces, dim):
+    shape = list(pieces.shape[1:])
+    shape[dim] *= pieces.shape[0]
+    return jnp.moveaxis(pieces, 0, dim).reshape(shape)
+
+
+def exchange_directly(x, axis, split_dim, concat_dim):
+    count, here = (lax.axis_size(axis), lax.axis_index(axis))
+    tiles = cut_along(x, split_dim, count)
+    done = [tiles[here]]
+    for step in range(1, count):
+        sent = tiles[(here + step) % count]
+        done.append(lax.ppermute(sent, axis, [(i, (i + step) % count) for i in range(count)]))
+    tiles = jnp.stack(done)[(here - jnp.arange(count)) % count]
+    return joined_along(tiles, concat_dim)
 
 
 def passed_along(block, axis, distance):
@@ -83,7 +105,7 @@
     column_cos, column_sin = angles(column_index[:, None] * column_index[None, :], shards, 1.0)
     pair = (
         lax.all_to_all(back_real, "seq", split_axis=2, concat_axis=1, tiled=True),
-        lax.all_to_all(back_imag, "seq", split_axis=2, concat_axis=1, tiled=True),
+        exchange_directly(back_imag, "seq", 2, 1),
     )
     inv_real, inv_imag = complex_mix("dk,rkmc->rdmc", column_cos, column_sin, pair[0], pair[1])
     factor = 0.5 / total

time: 131 us -> 125 us (0.954)
  waiting for transfers between devices: 77.2 us -> 60.1 us
  starting transfers between devices: 29.5 us -> 40.4 us
    ppermute x0 -> x7, starting transfers between devices: none -> 12.6 us  [exchange_directly(): lax.ppermute(sent, axis, [(i, (i + step) % count) for i in range(count)])]
    all_to_all x1, waiting for transfers between devices: 8.24 us -> 0.01 us  [body(): lax.all_to_all(back_real, 'seq', split_axis=2, concat_axis=1, tiled=True)]
    all_to_all x1 -> x0, waiting for transfers between devices: 8.02 us -> none  [body(): lax.all_to_all(back_imag, 'seq', split_axis=2, concat_axis=1, tiled=True)]
    all_to_all x1 -> x0, starting transfers between devices: 3.59 us -> none  [body(): lax.all_to_all(back_imag, 'seq', split_axis=2, concat_axis=1, tiled=True)]
    all_to_all x1, waiting for transfers between devices: 14.1 us -> 11.6 us  [body(): lax.all_to_all(packed, 'seq', split_axis=1, concat_axis=2, tiled=True)]
    ppermute x0 -> x7, waiting for transfers between devices: none -> 2.4 us  [exchange_directly(): lax.ppermute(sent, axis, [(i, (i + step) % count) for i in range(count)])]
    all_to_all x1, starting transfers between devices: 3.59 us -> 5.43 us  [body(): lax.all_to_all(packed, 'seq', split_axis=1, concat_axis=2, tiled=True)]
  transfers between devices with their start and end apart: 7 -> 13, of which waited for: 7 -> 7; matrix products, arithmetic and copies ran while one was open for 3% -> 4% of each run, Pallas kernels for 0% -> 0%
where the time goes in v1:
time: 125 us
  waiting for transfers between devices  60.1 us (48%)
  starting transfers between devices  40.4 us (32%)
  matrix products  12.4 us (10%)
  local copies, waits for them, and re-layouts  8.37 us (7%)
  other arithmetic  2.67 us (2%)
    all_to_all x1, waiting for transfers between devices, body(): lax.all_to_all(lifted, 'seq', split_axis=3, concat_axis=2, tiled=True)  19 us
    all_to_all x1, waiting for transfers between devices, body(): lax.all_to_all(real_part, 'seq', split_axis=2, concat_axis=3, tiled=True)  13.4 us
    all_to_all x1, waiting for transfers between devices, body(): lax.all_to_all(imag_part, 'seq', split_axis=2, concat_axis=3, tiled=True)  13.2 us
    ppermute x7, starting transfers between devices, exchange_directly(): lax.ppermute(sent, axis, [(i, (i + step) % count) for i in range(count)])  12.6 us
    all_to_all x1, waiting for transfers between devices, body(): lax.all_to_all(packed, 'seq', split_axis=1, concat_axis=2, tiled=True)  11.6 us
    all_to_all x1, starting transfers between devices, body(): lax.all_to_all(lifted, 'seq', split_axis=3, concat_axis=2, tiled=True)  6.6 us
    all_to_all x1, starting transfers between devices, body(): lax.all_to_all(packed, 'seq', split_axis=1, concat_axis=2, tiled=True)  5.43 us
    ppermute x1, starting transfers between devices, passed_along(): return lax.ppermute(block, axis, route)  4.9 us
  transfers between devices with their start and end apart: 13, of which 7 were waited for; matrix products, arithmetic and copies ran while one was open for 4% of the time, Pallas kernels for 0%

profile of v1, /device:TPU:0, one launch (start us, length us, event | category | flops | bytes accessed | tf_op | source)
XLA Modules:
  0.0 124.5 jit_solution(10978525015470905914)
XLA Ops:
  0.0 1.1 pad_maximum_fusion.1
  1.1 4.9 %collective-permute-start = (f32[3,2,256]{2,1,0:T(2,128)S(1)}, f32[3,2,256]{2,1,0:T(2,128)S(1)}, u32[]{:S(2)}, u32[]{:S(2)}) collective-permute-start(f32[3,2,256]{2,1,0:T(2,128)S(1)} %slice.97), channel_id=1, source_target_pairs={{0,4},{4,8},{8,12},{12,16},{16,20},{20,24},{24,28},{1,5},{5,9},{9,... | collective-permute-start | bytes 18440 | tf_op jit(solution)/shard_map/ppermute | solution.py:33
  8.6 1.5 %copy.82 = f32[2,3,1,128,256]{4,0,2,1,3:T(2,128)} copy(f32[2,3,1,128,256]{4,3,1,0,2:T(8,128)S(1)} %maximum_bitcast_fusion) | data formatting | bytes 1572864 | tf_op jit(solution)/shard_map/broadcast_in_dim | solution.py:70
  10.2 6.6 %all-to-all-start = ((f32[2,3,1,128,256]{4,0,2,1,3:T(2,128)}), f32[2,3,1,128,256]{4,0,2,1,3:T(2,128)S(1)}, u32[]{:S(2)}, u32[]{:S(2)}) async-start(f32[2,3,1,128,256]{4,0,2,1,3:T(2,128)} %copy.82), calls=%async_computation | async-start | bytes 1572864 | tf_op jit(solution)/shard_map/all_to_all | solution.py:73
  16.9 19.0 %all-to-all-done = f32[2,3,1,128,256]{4,0,2,1,3:T(2,128)S(1)} async-done(((f32[2,3,1,128,256]{4,0,2,1,3:T(2,128)}), f32[2,3,1,128,256]{4,0,2,1,3:T(2,128)S(1)}, u32[]{:S(2)}, u32[]{:S(2)}) %all-to-all-start) | async-done | bytes 786464 | tf_op jit(solution)/shard_map/all_to_all | solution.py:73
  39.3 1.0 copy.86
  40.3 3.5 %all-to-all-start.1 = ((f32[2,2,8,16,256]{4,3,1,0,2:T(8,128)}), f32[2,2,8,16,256]{4,3,1,0,2:T(8,128)S(1)}, u32[]{:S(2)}, u32[]{:S(2)}) async-start(f32[2,2,8,16,256]{4,3,1,0,2:T(8,128)} %copy.86), calls=%async_computation.1 | async-start | bytes 1048576 | tf_op jit(solution)/shard_map/all_to_all | solution.py:88
  44.8 13.4 %all-to-all-done.1 = f32[2,2,8,16,256]{4,3,1,0,2:T(8,128)S(1)} async-done(((f32[2,2,8,16,256]{4,3,1,0,2:T(8,128)}), f32[2,2,8,16,256]{4,3,1,0,2:T(8,128)S(1)}, u32[]{:S(2)}, u32[]{:S(2)}) %all-to-all-start.1) | async-done | bytes 524320 | tf_op jit(solution)/shard_map/all_to_all | solution.py:88
  58.2 3.7 %all-to-all-start.2 = ((f32[2,2,8,16,256]{4,3,1,0,2:T(8,128)}), f32[2,2,8,16,256]{4,3,1,0,2:T(8,128)S(1)}, u32[]{:S(2)}, u32[]{:S(2)}) async-start(f32[2,2,8,16,256]{4,3,1,0,2:T(8,128)} %copy.89), calls=%async_computation.2 | async-start | bytes 1048576 | tf_op jit(solution)/shard_map/all_to_all | solution.py:89
  62.1 1.1 fusion.46
  63.2 13.2 %all-to-all-done.2 = f32[2,2,8,16,256]{4,3,1,0,2:T(8,128)S(1)} async-done(((f32[2,2,8,16,256]{4,3,1,0,2:T(8,128)}), f32[2,2,8,16,256]{4,3,1,0,2:T(8,128)S(1)}, u32[]{:S(2)}, u32[]{:S(2)}) %all-to-all-start.2) | async-done | bytes 524320 | tf_op jit(solution)/shard_map/all_to_all | solution.py:89
  76.5 1.1 fusion.44
  77.6 1.1 fusion.3
  78.7 1.1 fusion.2
  82.6 1.5 %collective-permute-start.1 = (f32[2,1,16,256]{3,2,0,1:T(8,128)S(1)}, f32[2,1,16,256]{3,2,0,1:T(8,128)S(1)}, u32[]{:S(2)}, u32[]{:S(2)}) collective-permute-start(f32[2,1,16,256]{3,2,0,1:T(8,128)S(1)} %get-tuple-element.24), channel_id=1, source_target_pairs={{0,4},{4,8},{8,12},{12,16},{16,20},{20,24},{24,28},{28,0},{1,5},{5... | collective-permute-start | bytes 98312 | tf_op jit(solution)/shard_map/ppermute | solution.py:25
  84.1 1.8 %collective-permute-start.3 = (f32[2,1,16,256]{3,2,0,1:T(8,128)S(1)}, f32[2,1,16,256]{3,2,0,1:T(8,128)S(1)}, u32[]{:S(2)}, u32[]{:S(2)}) collective-permute-start(f32[2,1,16,256]{3,2,0,1:T(8,128)S(1)} %get-tuple-element.22), channel_id=1, source_target_pairs={{0,12},{4,16},{8,20},{12,24},{16,28},{20,0},{24,4},{28,8},{1,13},{... | collective-permute-start | bytes 98312 | tf_op jit(solution)/shard_map/ppermute | solution.py:25
  85.9 2.8 %collective-permute-start.4 = (f32[2,1,16,256]{3,2,0,1:T(8,128)S(1)}, f32[2,1,16,256]{3,2,0,1:T(8,128)S(1)}, u32[]{:S(2)}, u32[]{:S(2)}) collective-permute-start(f32[2,1,16,256]{3,2,0,1:T(8,128)S(1)} %get-tuple-element.21), channel_id=1, source_target_pairs={{0,16},{4,20},{8,24},{12,28},{16,0},{20,4},{24,8},{28,12},{1,17},{... | collective-permute-start | bytes 98312 | tf_op jit(solution)/shard_map/ppermute | solution.py:25
  88.7 1.3 %collective-permute-start.5 = (f32[2,1,16,256]{3,2,0,1:T(8,128)S(1)}, f32[2,1,16,256]{3,2,0,1:T(8,128)S(1)}, u32[]{:S(2)}, u32[]{:S(2)}) collective-permute-start(f32[2,1,16,256]{3,2,0,1:T(8,128)S(1)} %get-tuple-element.20), channel_id=1, source_target_pairs={{0,20},{4,24},{8,28},{12,0},{16,4},{20,8},{24,12},{28,16},{1,21},{... | collective-permute-start | bytes 98312 | tf_op jit(solution)/shard_map/ppermute | solution.py:25
  90.9 3.6 %all-to-all-start.3 = ((f32[2,1,128,256]{3,0,1,2:T(2,128)}), f32[2,1,128,256]{3,0,1,2:T(2,128)S(1)}, u32[]{:S(2)}, u32[]{:S(2)}) async-start(f32[2,1,128,256]{3,0,1,2:T(2,128)} %copy.98), calls=%async_computation.3 | async-start | bytes 524288 | tf_op jit(solution)/shard_map/all_to_all | solution.py:107
  94.5 3.8 %collective-permute-start.6 = (f32[2,1,16,256]{3,2,0,1:T(8,128)S(1)}, f32[2,1,16,256]{3,2,0,1:T(8,128)S(1)}, u32[]{:S(2)}, u32[]{:S(2)}) collective-permute-start(f32[2,1,16,256]{3,2,0,1:T(8,128)S(1)} %get-tuple-element.19), channel_id=1, source_target_pairs={{0,24},{4,28},{8,0},{12,4},{16,8},{20,12},{24,16},{28,20},{1,25},{... | collective-permute-start | bytes 98312 | tf_op jit(solution)/shard_map/ppermute | solution.py:25
  98.3 1.5 %collective-permute-start.7 = (f32[2,1,16,256]{3,2,0,1:T(8,128)S(1)}, f32[2,1,16,256]{3,2,0,1:T(8,128)S(1)}, u32[]{:S(2)}, u32[]{:S(2)}) collective-permute-start(f32[2,1,16,256]{3,2,0,1:T(8,128)S(1)} %get-tuple-element.18), channel_id=1, source_target_pairs={{0,28},{4,0},{8,4},{12,8},{16,12},{20,16},{24,20},{28,24},{1,29},{... | collective-permute-start | bytes 98312 | tf_op jit(solution)/shard_map/ppermute | solution.py:25
  99.9 2.3 %collective-permute-done.7 = f32[2,1,16,256]{3,2,0,1:T(8,128)S(1)} collective-permute-done((f32[2,1,16,256]{3,2,0,1:T(8,128)S(1)}, f32[2,1,16,256]{3,2,0,1:T(8,128)S(1)}, u32[]{:S(2)}, u32[]{:S(2)}) %collective-permute-start.7) | collective-permute-done | bytes 32800 | tf_op jit(solution)/shard_map/ppermute | solution.py:25
  106.0 5.4 %all-to-all-start.4 = ((f32[4,8,16,256]{3,2,0,1:T(8,128)}), f32[4,8,16,256]{3,2,0,1:T(8,128)S(1)}, u32[]{:S(2)}, u32[]{:S(2)}) async-start(f32[4,8,16,256]{3,2,0,1:T(8,128)} %copy.104), calls=%async_computation.4 | async-start | bytes 1048576 | tf_op jit(solution)/shard_map/all_to_all | solution.py:113
  111.5 11.6 %all-to-all-done.4 = f32[4,8,16,256]{3,2,0,1:T(8,128)S(1)} async-done(((f32[4,8,16,256]{3,2,0,1:T(8,128)}), f32[4,8,16,256]{3,2,0,1:T(8,128)S(1)}, u32[]{:S(2)}, u32[]{:S(2)}) %all-to-all-start.4) | async-done | bytes 524320 | tf_op jit(solution)/shard_map/all_to_all | solution.py:113
  (75 shorter events, 16.1 us)
Async XLA Ops:
  0.0 7.4 %copy-start = (f32[128,256]{1,0:T(8,128)S(1)}, f32[128,256]{1,0:T(8,128)}, u32[]{:S(2)}) copy-start(f32[128,256]{1,0:T(8,128)} %param.8) | copy-start | bytes 393220
  0.0 7.4 %copy-start.1 = (f32[128,256]{1,0:T(8,128)S(1)}, f32[128,256]{1,0:T(8,128)}, u32[]{:S(2)}) copy-start(f32[128,256]{1,0:T(8,128)} %param.7) | copy-start | bytes 393220
  0.0 7.4 %copy-start.2 = (f32[128,256]{1,0:T(8,128)S(1)}, f32[128,256]{1,0:T(8,128)}, u32[]{:S(2)}) copy-start(f32[128,256]{1,0:T(8,128)} %param.6) | copy-start | bytes 393220
  1.1 6.2 %collective-permute-start = (f32[3,2,256]{2,1,0:T(2,128)S(1)}, f32[3,2,256]{2,1,0:T(2,128)S(1)}, u32[]{:S(2)}, u32[]{:S(2)}) collective-permute-start(f32[3,2,256]{2,1,0:T(2,128)S(1)} %slice.97), channel_id=1, source_target_pairs={{0,4},{4,8},{8,12},{12,16},{16,20},{20,24},{24,28},{1,5},{5,9},{9,... | collective-permute-start | bytes 18440 | tf_op jit(solution)/shard_map/ppermute | solution.py:33
  6.0 0.7 copy-start.4
  7.5 0.9 copy-start.3
  10.2 25.7 %all-to-all-start = ((f32[2,3,1,128,256]{4,0,2,1,3:T(2,128)}), f32[2,3,1,128,256]{4,0,2,1,3:T(2,128)S(1)}, u32[]{:S(2)}, u32[]{:S(2)}) async-start(f32[2,3,1,128,256]{4,0,2,1,3:T(2,128)} %copy.82), calls=%async_computation | async-start | bytes 1572864 | tf_op jit(solution)/shard_map/all_to_all | solution.py:73
  40.3 17.9 %all-to-all-start.1 = ((f32[2,2,8,16,256]{4,3,1,0,2:T(8,128)}), f32[2,2,8,16,256]{4,3,1,0,2:T(8,128)S(1)}, u32[]{:S(2)}, u32[]{:S(2)}) async-start(f32[2,2,8,16,256]{4,3,1,0,2:T(8,128)} %copy.86), calls=%async_computation.1 | async-start | bytes 1048576 | tf_op jit(solution)/shard_map/all_to_all | solution.py:88
  58.2 18.3 %all-to-all-start.2 = ((f32[2,2,8,16,256]{4,3,1,0,2:T(8,128)}), f32[2,2,8,16,256]{4,3,1,0,2:T(8,128)S(1)}, u32[]{:S(2)}, u32[]{:S(2)}) async-start(f32[2,2,8,16,256]{4,3,1,0,2:T(8,128)} %copy.89), calls=%async_computation.2 | async-start | bytes 1048576 | tf_op jit(solution)/shard_map/all_to_all | solution.py:89
  82.6 11.9 %collective-permute-start.1 = (f32[2,1,16,256]{3,2,0,1:T(8,128)S(1)}, f32[2,1,16,256]{3,2,0,1:T(8,128)S(1)}, u32[]{:S(2)}, u32[]{:S(2)}) collective-permute-start(f32[2,1,16,256]{3,2,0,1:T(8,128)S(1)} %get-tuple-element.24), channel_id=1, source_target_pairs={{0,4},{4,8},{8,12},{12,16},{16,20},{20,24},{24,28},{28,0},{1,5},{5... | collective-permute-start | bytes 98312 | tf_op jit(solution)/shard_map/ppermute | solution.py:25
  84.1 14.2 %collective-permute-start.2 = (f32[2,1,16,256]{3,2,0,1:T(8,128)S(1)}, f32[2,1,16,256]{3,2,0,1:T(8,128)S(1)}, u32[]{:S(2)}, u32[]{:S(2)}) collective-permute-start(f32[2,1,16,256]{3,2,0,1:T(8,128)S(1)} %get-tuple-element.23), channel_id=1, source_target_pairs={{0,8},{4,12},{8,16},{12,20},{16,24},{20,28},{24,0},{28,4},{1,9},{5... | collective-permute-start | bytes 98312 | tf_op jit(solution)/shard_map/ppermute | solution.py:25
  84.1 15.7 %collective-permute-start.3 = (f32[2,1,16,256]{3,2,0,1:T(8,128)S(1)}, f32[2,1,16,256]{3,2,0,1:T(8,128)S(1)}, u32[]{:S(2)}, u32[]{:S(2)}) collective-permute-start(f32[2,1,16,256]{3,2,0,1:T(8,128)S(1)} %get-tuple-element.22), channel_id=1, source_target_pairs={{0,12},{4,16},{8,20},{12,24},{16,28},{20,0},{24,4},{28,8},{1,13},{... | collective-permute-start | bytes 98312 | tf_op jit(solution)/shard_map/ppermute | solution.py:25
  85.9 13.9 %collective-permute-start.4 = (f32[2,1,16,256]{3,2,0,1:T(8,128)S(1)}, f32[2,1,16,256]{3,2,0,1:T(8,128)S(1)}, u32[]{:S(2)}, u32[]{:S(2)}) collective-permute-start(f32[2,1,16,256]{3,2,0,1:T(8,128)S(1)} %get-tuple-element.21), channel_id=1, source_target_pairs={{0,16},{4,20},{8,24},{12,28},{16,0},{20,4},{24,8},{28,12},{1,17},{... | collective-permute-start | bytes 98312 | tf_op jit(solution)/shard_map/ppermute | solution.py:25
  88.7 11.1 %collective-permute-start.5 = (f32[2,1,16,256]{3,2,0,1:T(8,128)S(1)}, f32[2,1,16,256]{3,2,0,1:T(8,128)S(1)}, u32[]{:S(2)}, u32[]{:S(2)}) collective-permute-start(f32[2,1,16,256]{3,2,0,1:T(8,128)S(1)} %get-tuple-element.20), channel_id=1, source_target_pairs={{0,20},{4,24},{8,28},{12,0},{16,4},{20,8},{24,12},{28,16},{1,21},{... | collective-permute-start | bytes 98312 | tf_op jit(solution)/shard_map/ppermute | solution.py:25
  90.9 12.5 %all-to-all-start.3 = ((f32[2,1,128,256]{3,0,1,2:T(2,128)}), f32[2,1,128,256]{3,0,1,2:T(2,128)S(1)}, u32[]{:S(2)}, u32[]{:S(2)}) async-start(f32[2,1,128,256]{3,0,1,2:T(2,128)} %copy.98), calls=%async_computation.3 | async-start | bytes 524288 | tf_op jit(solution)/shard_map/all_to_all | solution.py:107
  94.5 5.4 %collective-permute-start.6 = (f32[2,1,16,256]{3,2,0,1:T(8,128)S(1)}, f32[2,1,16,256]{3,2,0,1:T(8,128)S(1)}, u32[]{:S(2)}, u32[]{:S(2)}) collective-permute-start(f32[2,1,16,256]{3,2,0,1:T(8,128)S(1)} %get-tuple-element.19), channel_id=1, source_target_pairs={{0,24},{4,28},{8,0},{12,4},{16,8},{20,12},{24,16},{28,20},{1,25},{... | collective-permute-start | bytes 98312 | tf_op jit(solution)/shard_map/ppermute | solution.py:25
  98.3 3.9 %collective-permute-start.7 = (f32[2,1,16,256]{3,2,0,1:T(8,128)S(1)}, f32[2,1,16,256]{3,2,0,1:T(8,128)S(1)}, u32[]{:S(2)}, u32[]{:S(2)}) collective-permute-start(f32[2,1,16,256]{3,2,0,1:T(8,128)S(1)} %get-tuple-element.18), channel_id=1, source_target_pairs={{0,28},{4,0},{8,4},{12,8},{16,12},{20,16},{24,20},{28,24},{1,29},{... | collective-permute-start | bytes 98312 | tf_op jit(solution)/shard_map/ppermute | solution.py:25
  106.0 17.0 %all-to-all-start.4 = ((f32[4,8,16,256]{3,2,0,1:T(8,128)}), f32[4,8,16,256]{3,2,0,1:T(8,128)S(1)}, u32[]{:S(2)}, u32[]{:S(2)}) async-start(f32[4,8,16,256]{3,2,0,1:T(8,128)} %copy.104), calls=%async_computation.4 | async-start | bytes 1048576 | tf_op jit(solution)/shard_map/all_to_all | solution.py:113
  123.1 0.7 copy-start.5
